TPU v7x, 32 devices: a whole 2x2x4 slice. The times are simulated.
32 devices in a mesh: expert: 8 (over z, x), dp: 4 (over y, core).
Axes of the slice: x: 2, y: 2, z: 4, core: 2. Of those that a mesh axis runs over, the one named last changes fastest.
Arguments:
- tokens: bfloat16 [4096, 2048], P(('expert', 'dp')), may hold values from -6 to 6
- routes: int32 [4096, 8], P(('expert', 'dp')), may hold values from 0 to 63, all different within a row; in each aligned block of 128 rows (0 to 127, 128 to 255, ...) at most 32 rows name the same one
- gates: float32 [4096, 8], P(('expert', 'dp')), may hold values from 0.1 to 1
- cotangent: bfloat16 [4096, 2048], P(('expert', 'dp')), may hold values from -6 to 6
- w_up: bfloat16 [64, 2048, 128], P('expert'), may hold values from -0.125 to 0.125
- w_down: bfloat16 [64, 128, 2048], P('expert'), may hold values from -0.5 to 0.5
Outputs:
- mixed: bfloat16 [4096, 2048], P(('expert', 'dp'))
- token_grad: bfloat16 [4096, 2048], P(('expert', 'dp'))
- grad_up: bfloat16 [64, 2048, 128], P('expert', 'dp')
- grad_down: bfloat16 [64, 128, 2048], P('expert', None, 'dp')
Inputs may be any that keep to these rules, and one draw needn't show every extreme that they name: `routes`: each row names 8 different experts; within the rows of one device no expert is named more than min(32, 128) times, and some expert is named exactly that often.
All inputs are finite; a program needn't handle non-finite values.
Results may differ from a plain program's by a relative error of at most 0.013.
Values may be sent and summed in bfloat16 or wider, within the bound.
A program may use at most 128 MiB of HBM per device.

v0:
```python
import functools

import jax
import jax.numpy as jnp
from jax import lax
from jax.experimental import pallas as pl
from jax.experimental.pallas import tpu as pltpu
from jax.sharding import PartitionSpec as P

gelu_coef = 0.7978845608028654
cubic_coef = 0.044715
MESH = pl.DeviceIdType.MESH
CORES = 2


def gelu_and_slope(pre_act):
    square = pre_act * pre_act
    tanh_part = jnp.tanh(gelu_coef * pre_act * (1.0 + cubic_coef * square))
    value = 0.5 * pre_act * (1.0 + tanh_part)
    slope = 0.5 * (1.0 + tanh_part) + 0.5 * pre_act * (1.0 - tanh_part * tanh_part) * gelu_coef * (
        1.0 + 3.0 * cubic_coef * square
    )
    return value, slope


def kept_gates(routes, gates, experts_all, capacity):
    tok_rows = routes.shape[0]
    hits = routes[:, :, None] == jnp.arange(experts_all, dtype=jnp.int32)[None, None, :]
    named = jnp.any(hits, axis=1)
    gate_of = jnp.sum(jnp.where(hits, gates[:, :, None], jnp.float32(0.0)), axis=1)
    earlier = jnp.tril(jnp.ones((tok_rows, tok_rows), jnp.bfloat16), -1)
    rank = jnp.dot(earlier, named.astype(jnp.bfloat16), preferred_element_type=jnp.float32)
    return jnp.where(named & (rank < capacity), gate_of, jnp.float32(0.0))


def dot_nn(a, b):
    return lax.dot_general(a, b, (((1,), (0,)), ((), ())), preferred_element_type=jnp.float32)


def dot_nt(a, b):
    return lax.dot_general(a, b, (((1,), (1,)), ((), ())), preferred_element_type=jnp.float32)


class Sizes:
    def __init__(self, n_expert, n_dp, tokens, routes, w_up):
        self.n_y = n_dp // CORES
        self.n_x = n_dp // CORES
        self.n_z = n_expert // self.n_x
        self.local, self.width, self.hidden = w_up.shape
        self.rows = tokens.shape[0]
        self.top = routes.shape[1]
        self.experts = self.local * n_expert
        self.capacity = self.rows * self.top // self.experts
        self.half = self.local * self.hidden
        self.units = self.half * self.n_x
        self.column = self.rows * self.n_z
        self.slice = self.width // n_dp
        self.lanes = 2 * self.experts
        self.tile = 2 * self.hidden
        self.tiles = self.half // self.tile
        self.share = self.local // n_dp


def step_kernel(
    s,
    tok_h, routes_ref, gates_ref, cot_h, up_h, down_h,
    mixed_o, tgrad_o, gup_o, gdown_o,
    X, C, G, WU, WD, HT, GP, MS, TS, MR, TR, SB, CR, XU, YD, YU, XD,
    lsem, tok_s, tok_r, cot_s, cot_r, gate_s, gate_r, wx_s, wx_r, wy_s, wy_r, wc_s, wc_r,
    m_s, m_r, g_s, g_r, core_s, core_r, xu_s, xu_r, yd_s, yd_r, xd_s, xd_r, yu_s, yu_r,
):
    e = lax.axis_index("expert")
    p = lax.axis_index("dp")
    z, x = e // s.n_x, e % s.n_x
    y, c = p // CORES, p % CORES
    T, H, F, D = s.rows, s.half, s.hidden, s.width
    tile, tiles, sl = s.tile, s.tiles, s.slice
    wide = s.n_y * sl

    def at(z_, x_, y_, c_):
        return (z_ * s.n_x + x_, y_ * CORES + c_)

    x_peer, y_peer, c_peer = at(z, 1 - x, y, c), at(z, x, 1 - y, c), at(z, x, y, 1 - c)

    def z_peer(zz):
        return at(zz, x, y, c)

    def remote(src, dst, send, recv, device):
        return pltpu.make_async_remote_copy(
            src_ref=src, dst_ref=dst, send_sem=send, recv_sem=recv, device_id=device, device_id_type=MESH
        )

    def up(n):
        return pl.multiple_of(n, 128)

    def block(ref, zz):
        return ref.at[pl.ds(up(zz * T), T)]

    own_up = [
        pltpu.make_async_copy(up_h.at[i], WU.at[:, pl.ds(up(x * H + i * F), F)], lsem.at[2 + i])
        for i in range(s.local)
    ]
    own_down = pltpu.make_async_copy(down_h, WD.at[pl.ds(up(x * H), H)], lsem.at[2 + s.local])
    own_tok = pltpu.make_async_copy(tok_h, block(X, z), lsem.at[0])
    own_cot = pltpu.make_async_copy(cot_h, block(C, z), lsem.at[1])

    barrier = pltpu.get_barrier_semaphore()
    peers = [z_peer((z + k) % s.n_z) for k in range(1, s.n_z)] + [x_peer, y_peer, c_peer]
    for peer in peers:
        pl.semaphore_signal(barrier, inc=1, device_id=peer, device_id_type=MESH)
    own_tok.start()
    own_cot.start()
    for item in own_up:
        item.start()
    own_down.start()
    pl.semaphore_wait(barrier, len(peers))

    has_right, has_left = z < s.n_z - 1, z > 0
    right, left = jnp.minimum(z + 1, s.n_z - 1), jnp.maximum(z - 1, 0)

    def own_block(which, src, ref, send, recv, device):
        return remote(src, block(ref, z), send.at[which], recv.at[z], device)

    first_x = (y * CORES + c) * s.share

    def weight_at(u, x_, base):
        i = base + u // 2
        if u % 2 == 0:
            return WU.at[:, pl.ds(up(x_ * H + i * F), F)]
        return WD.at[pl.ds(up(x_ * H + i * F), F)]

    def weight_from(u):
        i = first_x + u // 2
        if u % 2 == 0:
            return up_h.at[i]
        return down_h.at[pl.ds(up(i * F), F)]

    n_w = 2 * s.share
    base_y = ((1 - y) * CORES + c) * s.share
    wx_send = [
        remote(weight_from(u), weight_at(u, x, first_x), wx_s.at[u], wx_r.at[u], x_peer) for u in range(n_w)
    ]
    wx_in = [
        remote(weight_from(u), weight_at(u, 1 - x, first_x), wx_s.at[u], wx_r.at[u], x_peer)
        for u in range(n_w)
    ]
    wy_send = [
        remote(weight_at(u, 1 - x, first_x), weight_at(u, 1 - x, first_x), wy_s.at[u], wy_r.at[u], y_peer)
        for u in range(n_w)
    ]
    wy_in = [
        remote(weight_at(u, 1 - x, base_y), weight_at(u, 1 - x, base_y), wy_s.at[u], wy_r.at[u], y_peer)
        for u in range(n_w)
    ]
    other_x = (y * CORES + 1 - c) * s.share
    other_y = ((1 - y) * CORES + 1 - c) * s.share
    wc_send = [
        remote(weight_at(u, 1 - x, b), weight_at(u, 1 - x, b), wc_s.at[k * n_w + u], wc_r.at[k * n_w + u], c_peer)
        for k, b in enumerate((first_x, base_y))
        for u in range(n_w)
    ]
    wc_in = [
        remote(weight_at(u, 1 - x, b), weight_at(u, 1 - x, b), wc_s.at[k * n_w + u], wc_r.at[k * n_w + u], c_peer)
        for k, b in enumerate((other_x, other_y))
        for u in range(n_w)
    ]

    @pl.when(has_right)
    def _():
        own_block(0, tok_h, X, tok_s, tok_r, z_peer(right)).start()
        own_block(0, cot_h, C, cot_s, cot_r, z_peer(right)).start()

    @pl.when(has_left)
    def _():
        own_block(1, tok_h, X, tok_s, tok_r, z_peer(left)).start()
        own_block(1, cot_h, C, cot_s, cot_r, z_peer(left)).start()

    for item in wx_send:
        item.start()

    E = s.experts
    lane = lax.broadcasted_iota(jnp.int32, (T, s.lanes), 1)
    expert = jnp.where(lane >= E, lane - E, lane)
    routes, gates = routes_ref[...], gates_ref[...]
    gate_of = jnp.zeros((T, s.lanes), jnp.float32)
    count = jnp.zeros((T, s.lanes), jnp.float32)
    for k in range(s.top):
        hit = routes[:, k : k + 1] == expert
        gate_of = gate_of + jnp.where(hit, gates[:, k : k + 1], 0.0)
        count = count + jnp.where(hit, 1.0, 0.0)
    tr = lax.broadcasted_iota(jnp.int32, (T, T), 0)
    tc = lax.broadcasted_iota(jnp.int32, (T, T), 1)
    earlier = jnp.where(tc < tr, 1.0, 0.0).astype(jnp.bfloat16)
    rank = dot_nn(earlier, count.astype(jnp.bfloat16))
    kept = jnp.where((count > 0.5) & (rank < s.capacity), gate_of, 0.0)
    high = kept.astype(jnp.bfloat16).astype(jnp.float32)
    G[pl.ds(up(z * T), T), :] = jnp.where(lane >= E, kept - high, high).astype(jnp.bfloat16)

    def gate_copy(k):
        peer = (z + k) % s.n_z
        return remote(block(G, z), block(G, z), gate_s.at[k], gate_r.at[z], z_peer(peer))

    def gate_in(zz):
        remote(block(G, zz), block(G, zz), gate_s.at[0], gate_r.at[zz], z_peer(z)).wait_recv()

    near = z + 1 - 2 * (z % 2)
    second = jnp.where(z < s.n_z // 2, s.n_z // 2, s.n_z // 2 - 1)
    last = jnp.where(z < s.n_z // 2, s.n_z - 1, 0)
    inner = has_right & has_left

    def arrive(k, src, ref, send, recv):
        remote(block(ref, src), block(ref, src), send.at[1 + k], recv.at[src], z_peer(z)).wait_recv()
        onward = jnp.where(src < z, z + 1, z - 1)
        ok = (onward >= 0) & (onward < s.n_z)
        goal = jnp.clip(onward, 0, s.n_z - 1)

        @pl.when(ok)
        def _():
            remote(block(ref, src), block(ref, src), send.at[1 + k], recv.at[src], z_peer(goal)).start()

    def arrived_sends(k, src, ref, send, recv):
        onward = jnp.where(src < z, z + 1, z - 1)
        ok = (onward >= 0) & (onward < s.n_z)

        @pl.when(ok)
        def _():
            remote(block(ref, src), block(ref, src), send.at[1 + k], recv.at[src], z_peer(z)).wait_send()

    def weight_x(u):
        wx_in[u].wait_recv()
        wy_send[u].start()
        wc_send[u].start()

    def weight_y(u):
        wy_in[u].wait_recv()
        wc_send[n_w + u].start()

    def units(row0, count_rows, tile0, n_tiles):
        rows = pl.ds(up(row0), count_rows)

        @pl.loop(0, n_tiles)
        def _(n):
            u0 = up((tile0 + n) * tile)
            cols = pl.ds(u0, tile)
            first = z * s.n_x * s.local + (tile0 + n) * (tile // F)
            ri = lax.broadcasted_iota(jnp.int32, (s.lanes, tile), 0)
            ci = lax.broadcasted_iota(jnp.int32, (s.lanes, tile), 1)
            goal = first + jnp.where(ci >= F, 1, 0)
            pick = jnp.where((ri == goal) | (ri == goal + E), 1.0, 0.0).astype(jnp.bfloat16)
            gate = dot_nn(G[rows, :], pick)
            pre = dot_nn(X[rows, :], WU[:, cols])
            value, slope = gelu_and_slope(pre)
            HT[rows, cols] = (value * gate).astype(jnp.bfloat16)
            grad_hidden = dot_nt(C[rows, :], WD[cols, :])
            GP[rows, cols] = (grad_hidden * (slope * gate)).astype(jnp.bfloat16)

    def mix(row0, count_rows):
        rows = pl.ds(up(row0), count_rows)

        @pl.loop(0, D // tile)
        def _(n):
            cols = pl.ds(up(n * tile), tile)
            MS[rows, cols] = dot_nn(HT[rows, :], WD[:, cols]).astype(jnp.bfloat16)

    def grads(row0, count_rows):
        rows = pl.ds(up(row0), count_rows)

        @pl.loop(0, D // tile)
        def _(n):
            cols = pl.ds(up(n * tile), tile)
            TS[rows, cols] = dot_nt(GP[rows, :], WU[cols, :]).astype(jnp.bfloat16)

    def give(k, dst, ref, into, send, recv):
        return remote(block(ref, dst), into.at[pl.ds(up(z * T), T)], send.at[k], recv.at[z], z_peer(dst))

    own_tok.wait()
    own_cot.wait()
    for k in range(1, s.n_z):
        gate_copy(k).start()
    for item in own_up:
        item.wait()
    own_down.wait()

    weight_x(0)
    arrive(1, near, X, tok_s, tok_r)
    weight_x(1)
    arrive(1, near, C, cot_s, cot_r)
    weight_y(0)
    arrive(2, second, X, tok_s, tok_r)
    weight_x(2)
    weight_y(1)
    arrive(2, second, C, cot_s, cot_r)
    gate_in(near)
    gate_in(second)
    gate_in(last)
    weight_x(3)
    weight_y(2)

    @pl.when(inner)
    def _():
        arrive(3, last, X, tok_s, tok_r)

    near_rows = jnp.where(z < s.n_z // 2, 0, T)
    count_rows = (s.n_z - 1) * T
    units(near_rows, count_rows, x * tiles, tiles)

    @pl.when(inner)
    def _():
        arrive(3, last, C, cot_s, cot_r)

    weight_y(3)
    for item in wc_in:
        item.wait_recv()
    units(near_rows, count_rows, (1 - x) * tiles, tiles)
    mix(near_rows, count_rows)
    give(0, near, MS, MR, m_s, m_r).start()
    give(1, second, MS, MR, m_s, m_r).start()
    grads(near_rows, count_rows)
    give(0, near, TS, TR, g_s, g_r).start()
    give(1, second, TS, TR, g_s, g_r).start()

    @pl.when(jnp.logical_not(inner))
    def _():
        arrive(3, last, X, tok_s, tok_r)
        arrive(3, last, C, cot_s, cot_r)

    units(last * T, T, 0, s.n_x * tiles)
    mix(last * T, T)
    give(2, last, MS, MR, m_s, m_r).start()

    for item in wy_send + wc_send:
        item.wait_send()
    Q = WD
    steps = s.n_x * tiles

    def unit_rows(i):
        side = jnp.where(i < tiles, 1 - x, x)
        return up(side * H + (i % tiles) * tile)

    def core_copy(i):
        rows = pl.ds(unit_rows(i), tile)
        return remote(SB.at[i % 2], CR.at[rows], core_s.at[i], core_r.at[i], c_peer)

    def xu_copy(i):
        return remote(
            Q.at[pl.ds(unit_rows(i), tile), pl.ds(0, wide)], XU.at[pl.ds(up(i * tile), tile)],
            xu_s.at[i], xu_r.at[i], x_peer,
        )

    def yd_copy(i):
        return remote(
            Q.at[pl.ds(unit_rows(i), tile), pl.ds(up(wide + (1 - y) * sl), sl)],
            YD.at[pl.ds(up(i * tile), tile)], yd_s.at[i], yd_r.at[i], y_peer,
        )

    def xd_copy(j):
        return remote(
            Q.at[pl.ds(up((1 - x) * H + j * tile), tile), pl.ds(up(wide + y * sl), sl)],
            XD.at[pl.ds(up(j * tile), tile)], xd_s.at[j], xd_r.at[j], x_peer,
        )

    def yu_copy(j):
        return remote(
            Q.at[pl.ds(up(x * H + j * tile), tile), pl.ds(up((1 - y) * sl), sl)],
            YU.at[pl.ds(up(j * tile), tile)], yu_s.at[j], yu_r.at[j], y_peer,
        )

    @pl.loop(0, steps + 1)
    def _(i):
        @pl.when(i < steps)
        def _():
            @pl.when(i >= 2)
            def _():
                core_copy(jnp.maximum(i - 2, 0)).wait_send()

            r0 = unit_rows(i)
            rows = pl.ds(r0, tile)
            slot = i % 2
            grad_t = GP[:, rows].T
            hid_t = HT[:, rows].T
            for yy in range(s.n_y):
                for arr, (left_t, right_ref) in enumerate(((grad_t, X), (hid_t, C))):
                    to = pl.ds((arr * s.n_y + yy) * sl, sl)
                    theirs = pl.ds(up((yy * CORES + 1 - c) * sl), sl)
                    mine = pl.ds(up((yy * CORES + c) * sl), sl)
                    SB[slot, :, to] = dot_nn(left_t, right_ref[:, theirs]).astype(jnp.bfloat16)
                    Q[rows, to] = dot_nn(left_t, right_ref[:, mine]).astype(jnp.bfloat16)
            core_copy(i).start()

        @pl.when(i >= 1)
        def _():
            j = jnp.maximum(i - 1, 0)
            core_copy(j).wait_recv()
            rows = pl.ds(unit_rows(j), tile)
            Q[rows, :] = (Q[rows, :].astype(jnp.float32) + CR[rows, :].astype(jnp.float32)).astype(jnp.bfloat16)

            @pl.when(j < tiles)
            def _():
                xu_copy(j).start()

            yd_copy(j).start()

    core_copy(steps - 2).wait_send()
    core_copy(steps - 1).wait_send()

    grads(last * T, T)
    give(2, last, TS, TR, g_s, g_r).start()

    @pl.loop(0, tiles)
    def _(j):
        yd_copy(j).wait_recv()
        rows = pl.ds(up((1 - x) * H + j * tile), tile)
        cols = pl.ds(up(wide + y * sl), sl)
        got = YD[pl.ds(up(j * tile), tile), :]
        Q[rows, cols] = (Q[rows, cols].astype(jnp.float32) + got.astype(jnp.float32)).astype(jnp.bfloat16)
        xd_copy(j).start()

    @pl.loop(0, tiles)
    def _(j):
        xu_copy(j).wait_recv()
        rows = pl.ds(up(x * H + j * tile), tile)
        cols = pl.ds(0, wide)
        got = XU[pl.ds(up(j * tile), tile), :]
        Q[rows, cols] = (Q[rows, cols].astype(jnp.float32) + got.astype(jnp.float32)).astype(jnp.bfloat16)
        yu_copy(j).start()

    def taken(src, into, recv):
        remote(block(into, src), block(into, src), recv.at[src], recv.at[src], z_peer(z)).wait_recv()

    def total(out, own, part, into, recv):
        for src in (near, second, last):
            taken(src, into, recv)
        value = own[pl.ds(up(z * T), T), :].astype(jnp.float32) + part[pl.ds(up(z * T), T), :].astype(jnp.float32)
        for src in (near, second, last):
            value = value + into[pl.ds(up(src * T), T), :].astype(jnp.float32)
        out[...] = value.astype(jnp.bfloat16)

    total(mixed_o, X, MS, MR, m_r)
    total(tgrad_o, C, TS, TR, g_r)

    @pl.loop(0, tiles)
    def _(j):
        yd_copy(tiles + j).wait_recv()
        xd_copy(j).wait_recv()
        rows = pl.ds(up(x * H + j * tile), tile)
        piece = pl.ds(up(j * tile), tile)
        gdown_o[piece, :] = (
            Q[rows, pl.ds(up(wide + y * sl), sl)].astype(jnp.float32)
            + YD[pl.ds(up((tiles + j) * tile), tile), :].astype(jnp.float32)
            + XD[piece, :].astype(jnp.float32)
        ).astype(jnp.bfloat16)
        yu_copy(j).wait_recv()
        gup_o[piece, :] = (
            Q[rows, pl.ds(up(y * sl), sl)].astype(jnp.float32) + YU[piece, :].astype(jnp.float32)
        ).astype(jnp.bfloat16)

    @pl.when(has_right)
    def _():
        own_block(0, tok_h, X, tok_s, tok_r, z_peer(right)).wait_send()
        own_block(0, cot_h, C, cot_s, cot_r, z_peer(right)).wait_send()

    @pl.when(has_left)
    def _():
        own_block(1, tok_h, X, tok_s, tok_r, z_peer(left)).wait_send()
        own_block(1, cot_h, C, cot_s, cot_r, z_peer(left)).wait_send()

    for k, src in ((1, near), (2, second), (3, last)):
        arrived_sends(k, src, X, tok_s, tok_r)
        arrived_sends(k, src, C, cot_s, cot_r)
    for k in range(1, s.n_z):
        gate_copy(k).wait_send()
    for item in wx_send:
        item.wait_send()
    for k, dst in ((0, near), (1, second), (2, last)):
        give(k, dst, MS, MR, m_s, m_r).wait_send()
        give(k, dst, TS, TR, g_s, g_r).wait_send()

    @pl.loop(0, tiles)
    def _(j):
        xu_copy(j).wait_send()
        xd_copy(j).wait_send()
        yu_copy(j).wait_send()

    @pl.loop(0, steps)
    def _(j):
        yd_copy(j).wait_send()


def per_device(tokens, routes, gates, cotangent, w_up, w_down):
    s = Sizes(lax.axis_size("expert"), lax.axis_size("dp"), tokens, routes, w_up)
    bf = jnp.bfloat16
    dma = pltpu.SemaphoreType.DMA
    wide = s.n_y * s.slice
    n_w = 2 * s.share
    steps = s.n_x * s.tiles
    scratch = [
        pltpu.VMEM((s.column, s.width), bf),
        pltpu.VMEM((s.column, s.width), bf),
        pltpu.VMEM((s.column, s.lanes), bf),
        pltpu.VMEM((s.width, s.units), bf),
        pltpu.VMEM((s.units, s.width), bf),
        pltpu.VMEM((s.column, s.units), bf),
        pltpu.VMEM((s.column, s.units), bf),
        pltpu.VMEM((s.column, s.width), bf),
        pltpu.VMEM((s.column, s.width), bf),
        pltpu.VMEM((s.column, s.width), bf),
        pltpu.VMEM((s.column, s.width), bf),
        pltpu.VMEM((2, s.tile, 2 * wide), bf),
        pltpu.VMEM((s.units, 2 * wide), bf),
        pltpu.VMEM((s.half, wide), bf),
        pltpu.VMEM((s.units, s.slice), bf),
        pltpu.VMEM((s.half, s.slice), bf),
        pltpu.VMEM((s.half, s.slice), bf),
        dma((3 + s.local,)),
        dma((5,)), dma((s.n_z,)), dma((5,)), dma((s.n_z,)), dma((s.n_z,)), dma((s.n_z,)),
        dma((n_w,)), dma((n_w,)), dma((n_w,)), dma((n_w,)), dma((2 * n_w,)), dma((2 * n_w,)),
        dma((3,)), dma((s.n_z,)), dma((3,)), dma((s.n_z,)),
        dma((steps,)), dma((steps,)),
        dma((s.tiles,)), dma((s.tiles,)), dma((steps,)), dma((steps,)),
        dma((s.tiles,)), dma((s.tiles,)), dma((s.tiles,)), dma((s.tiles,)),
    ]
    any_space = pl.BlockSpec(memory_space=pl.ANY)
    vmem = pl.BlockSpec(memory_space=pltpu.VMEM)
    mixed, token_grad, grad_up, grad_down = pl.pallas_call(
        functools.partial(step_kernel, s),
        out_shape=(
            jax.ShapeDtypeStruct(tokens.shape, bf),
            jax.ShapeDtypeStruct(tokens.shape, bf),
            jax.ShapeDtypeStruct((s.half, s.slice), bf),
            jax.ShapeDtypeStruct((s.half, s.slice), bf),
        ),
        in_specs=[any_space, vmem, vmem, any_space, any_space, any_space],
        out_specs=(vmem, vmem, vmem, vmem),
        scratch_shapes=scratch,
        compiler_params=pltpu.CompilerParams(
            collective_id=0, has_side_effects=True, vmem_limit_bytes=67043328
        ),
        name="moe_step",
    )(tokens, routes, gates, cotangent, w_up, w_down.reshape(s.half, s.width))
    grad_up = grad_up.reshape(s.local, s.hidden, s.slice).transpose(0, 2, 1)
    return mixed, token_grad, grad_up, grad_down.reshape(s.local, s.hidden, s.slice)


def per_device_wide(tokens, routes, gates, cotangent, w_up, w_down):
    n_expert = lax.axis_size("expert")
    local_experts, model_width, hidden_width = w_up.shape
    experts_all = local_experts * n_expert
    tok_rows = tokens.shape[0]
    top_k = routes.shape[1]
    capacity = tok_rows * top_k // experts_all
    rows_all = n_expert * tok_rows
    units = local_experts * hidden_width

    gate_full = kept_gates(routes, gates, experts_all, capacity)
    gate_hi = gate_full.astype(jnp.bfloat16)
    gate_lo = (gate_full - gate_hi.astype(jnp.float32)).astype(jnp.bfloat16)
    gate_pair = jnp.concatenate([gate_hi, gate_lo], axis=1)

    all_tokens = lax.all_gather(tokens, "expert", axis=0, tiled=True)
    all_cot = lax.all_gather(
        jnp.concatenate([cotangent, gate_pair], axis=1), "expert", axis=0, tiled=True
    )
    first = lax.axis_index("expert") * local_experts
    all_gates = lax.dynamic_slice_in_dim(
        all_cot, model_width + first, local_experts, axis=1
    ).astype(jnp.float32) + lax.dynamic_slice_in_dim(
        all_cot, model_width + experts_all + first, local_experts, axis=1
    ).astype(jnp.float32)
    all_cot = all_cot[:, :model_width]
    gate_units = all_gates[:, :, None]

    pre_act = jnp.einsum("td,edf->tef", all_tokens, w_up, preferred_element_type=jnp.float32)
    value, slope = gelu_and_slope(pre_act)
    weighted = (value * gate_units).astype(jnp.bfloat16)
    mixed_part = jnp.einsum(
        "tef,efd->td", weighted, w_down, preferred_element_type=jnp.float32
    ).astype(jnp.bfloat16)
    mixed_sum = lax.psum_scatter(mixed_part, "expert", scatter_dimension=0, tiled=True)

    grad_hidden = jnp.einsum("td,efd->tef", all_cot, w_down, preferred_element_type=jnp.float32)
    grad_pre = (grad_hidden * slope * gate_units).astype(jnp.bfloat16)
    grad_part = jnp.einsum(
        "tef,edf->td", grad_pre, w_up, preferred_element_type=jnp.float32
    ).astype(jnp.bfloat16)
    grad_sum = lax.psum_scatter(grad_part, "expert", scatter_dimension=0, tiled=True)

    part_up = jnp.einsum(
        "td,tef->edf", all_tokens, grad_pre, preferred_element_type=jnp.float32
    ).astype(jnp.bfloat16)
    part_down = jnp.einsum(
        "tef,td->efd", weighted, all_cot, preferred_element_type=jnp.float32
    ).astype(jnp.bfloat16)
    up_sum = lax.psum_scatter(part_up, "dp", scatter_dimension=1, tiled=True)
    down_sum = lax.psum_scatter(part_down, "dp", scatter_dimension=2, tiled=True)

    mixed = (tokens.astype(jnp.float32) + mixed_sum.astype(jnp.float32)).astype(jnp.bfloat16)
    token_grad = (cotangent.astype(jnp.float32) + grad_sum.astype(jnp.float32)).astype(
        jnp.bfloat16
    )
    return (mixed, token_grad, up_sum, down_sum)


def solution(mesh):
    n_expert, n_dp = mesh.shape["expert"], mesh.shape["dp"]
    small = n_expert == 8 and n_dp == 4
    return jax.shard_map(
        per_device if small else per_device_wide,
        mesh=mesh,
        in_specs=(
            P(("expert", "dp"), None),
            P(("expert", "dp"), None),
            P(("expert", "dp"), None),
            P(("expert", "dp"), None),
            P("expert", None, None),
            P("expert", None, None),
        ),
        out_specs=(
            P(("expert", "dp"), None),
            P(("expert", "dp"), None),
            P("expert", "dp", None),
            P("expert", None, "dp"),
        ),
        check_vma=False,
    )
```

profile of v0, /device:TPU:0, one launch (start us, length us, event | category | flops | bytes accessed | tf_op | source)
XLA Modules:
  0.0 180.6 jit_solution(15988258058948873975)
XLA Ops:
  0.6 1.4 copy.10.routes_ref
  2.0 1.4 copy.11.gates_ref
  3.5 170.0 %moe_step.1 = (bf16[128,2048]{1,0:T(8,128)(2,1)}, bf16[128,2048]{1,0:T(8,128)(2,1)}, bf16[1024,512]{1,0:T(8,128)(2,1)}, bf16[1024,512]{1,0:T(8,128)(2,1)}) custom-call(bf16[128,2048]{1,0:T(8,128)(2,1)} %tok_h.1, s32[128,8]{1,0:T(8,128)} %copy.10.routes_ref, f32[128,8]{1,0:T(8,128)} %copy.11.gates_ref, bf16[128,2048]{1,0:T(8,128)(2,1)} %cot_h.1, ...), custom_call_target="tpu_custom_call" | custom-call | tf_op jit(solution)/shard_map/moe_step/pallas_call | solution.py:524
  173.5 0.0 copy-start
  173.5 2.3 %copy.12 = bf16[8,128,512]{1,2,0:T(8,128)(2,1)} copy(bf16[8,128,512]{2,1,0:T(8,128)(2,1)} %bitcast.7) | data formatting | bytes 2097152 | tf_op jit(solution)/shard_map/reshape | solution.py:540
  175.9 1.9 %copy.16 = bf16[128,2048]{1,0:T(8,128)(2,1)} copy(bf16[128,2048]{1,0:T(8,128)(2,1)} %get-tuple-element.16) | data formatting | bytes 1048576
  177.8 1.9 %copy.17 = bf16[128,2048]{1,0:T(8,128)(2,1)} copy(bf16[128,2048]{1,0:T(8,128)(2,1)} %get-tuple-element.17) | data formatting | bytes 1048576
  179.6 0.0 copy-done
  179.6 1.0 copy.18
Async XLA Ops:
  173.5 6.1 %copy-start = (bf16[1024,512]{1,0:T(8,128)(2,1)S(1)}, bf16[1024,512]{1,0:T(8,128)(2,1)}, u32[]{:S(2)}) copy-start(bf16[1024,512]{1,0:T(8,128)(2,1)} %get-tuple-element.11) | copy-start | bytes 3145732
where the time goes:
time: 181 us
  Pallas kernels  170 us (94%)
  local copies, waits for them, and re-layouts  9.91 us (5%)
    pallas_call x1, Pallas kernels, per_device(): pl.pallas_call(functools.partial(step_kernel, s), out_shape=(jax.ShapeDty...  170 us
    unnamed x7, local copies, waits for them, and re-layouts  7.57 us

commit v1 on v0

--- a/solution.py
+++ b/solution.py
@@ -63,10 +63,11 @@
 
 def step_kernel(
     s,
-    tok_h, routes_ref, gates_ref, cot_h, up_h, down_h,
-    mixed_o, tgrad_o, gup_o, gdown_o,
-    X, C, G, WU, WD, HT, GP, MS, TS, MR, TR, SB, CR, XU, YD, YU, XD,
-    lsem, tok_s, tok_r, cot_s, cot_r, gate_s, gate_r, wx_s, wx_r, wy_s, wy_r, wc_s, wc_r,
+    tok_h, routes_h, gates_h, cot_h, up_h, down_h,
+    mixed_h, tgrad_h, gup_h, gdown_h,
+    X, C, G, WU, WD, HT, GP, SL, MS, TS, MN, MP, MR, TN, TP, TR, Q, SB, CR, XU, YD, YU, XD,
+    mixed_o, tgrad_o, gup_o, gdown_o, routes_v, gates_v,
+    lsem, osem, tok_s, tok_r, cot_s, cot_r, gate_s, gate_r, wx_s, wx_r, wy_s, wy_r, wc_s, wc_r,
     m_s, m_r, g_s, g_r, core_s, core_r, xu_s, xu_r, yd_s, yd_r, xd_s, xd_r, yu_s, yu_r,
 ):
     e = lax.axis_index("expert")
@@ -75,6 +76,7 @@
     y, c = p // CORES, p % CORES
     T, H, F, D = s.rows, s.half, s.hidden, s.width
     tile, tiles, sl = s.tile, s.tiles, s.slice
+    steps = s.n_x * tiles
     wide = s.n_y * sl
 
     def at(z_, x_, y_, c_):
@@ -103,11 +105,15 @@
     own_down = pltpu.make_async_copy(down_h, WD.at[pl.ds(up(x * H), H)], lsem.at[2 + s.local])
     own_tok = pltpu.make_async_copy(tok_h, block(X, z), lsem.at[0])
     own_cot = pltpu.make_async_copy(cot_h, block(C, z), lsem.at[1])
+    own_routes = pltpu.make_async_copy(routes_h, routes_v, lsem.at[3 + s.local])
+    own_gates = pltpu.make_async_copy(gates_h, gates_v, lsem.at[4 + s.local])
 
     barrier = pltpu.get_barrier_semaphore()
     peers = [z_peer((z + k) % s.n_z) for k in range(1, s.n_z)] + [x_peer, y_peer, c_peer]
     for peer in peers:
         pl.semaphore_signal(barrier, inc=1, device_id=peer, device_id_type=MESH)
+    own_routes.start()
+    own_gates.start()
     own_tok.start()
     own_cot.start()
     for item in own_up:
@@ -178,23 +184,24 @@
     for item in wx_send:
         item.start()
 
+    own_routes.wait()
+    own_gates.wait()
     E = s.experts
-    lane = lax.broadcasted_iota(jnp.int32, (T, s.lanes), 1)
-    expert = jnp.where(lane >= E, lane - E, lane)
-    routes, gates = routes_ref[...], gates_ref[...]
-    gate_of = jnp.zeros((T, s.lanes), jnp.float32)
-    count = jnp.zeros((T, s.lanes), jnp.float32)
+    line = lax.broadcasted_iota(jnp.int32, (s.lanes, T), 0)
+    expert = jnp.where(line >= E, line - E, line)
+    gate_of = jnp.zeros((s.lanes, T), jnp.float32)
+    count = jnp.zeros((s.lanes, T), jnp.float32)
     for k in range(s.top):
-        hit = routes[:, k : k + 1] == expert
-        gate_of = gate_of + jnp.where(hit, gates[:, k : k + 1], 0.0)
+        hit = routes_v[k : k + 1, :] == expert
+        gate_of = gate_of + jnp.where(hit, gates_v[k : k + 1, :], 0.0)
         count = count + jnp.where(hit, 1.0, 0.0)
     tr = lax.broadcasted_iota(jnp.int32, (T, T), 0)
     tc = lax.broadcasted_iota(jnp.int32, (T, T), 1)
-    earlier = jnp.where(tc < tr, 1.0, 0.0).astype(jnp.bfloat16)
-    rank = dot_nn(earlier, count.astype(jnp.bfloat16))
+    earlier = jnp.where(tr < tc, 1.0, 0.0).astype(jnp.bfloat16)
+    rank = dot_nn(count.astype(jnp.bfloat16), earlier)
     kept = jnp.where((count > 0.5) & (rank < s.capacity), gate_of, 0.0)
     high = kept.astype(jnp.bfloat16).astype(jnp.float32)
-    G[pl.ds(up(z * T), T), :] = jnp.where(lane >= E, kept - high, high).astype(jnp.bfloat16)
+    G[pl.ds(up(z * T), T), :] = jnp.where(line >= E, kept - high, high).T.astype(jnp.bfloat16)
 
     def gate_copy(k):
         peer = (z + k) % s.n_z
@@ -235,43 +242,68 @@
         wy_in[u].wait_recv()
         wc_send[n_w + u].start()
 
-    def units(row0, count_rows, tile0, n_tiles):
-        rows = pl.ds(up(row0), count_rows)
-
-        @pl.loop(0, n_tiles)
+    def gate_tile(rows, t):
+        first = z * s.n_x * s.local + t * (tile // F)
+        ri = lax.broadcasted_iota(jnp.int32, (s.lanes, tile), 0)
+        ci = lax.broadcasted_iota(jnp.int32, (s.lanes, tile), 1)
+        goal = first + jnp.where(ci >= F, 1, 0)
+        pick = jnp.where((ri == goal) | (ri == goal + E), 1.0, 0.0).astype(jnp.bfloat16)
+        return dot_nn(G[rows, :], pick)
+
+    def units(rows, tile0):
+        @pl.loop(0, tiles)
         def _(n):
-            u0 = up((tile0 + n) * tile)
-            cols = pl.ds(u0, tile)
-            first = z * s.n_x * s.local + (tile0 + n) * (tile // F)
-            ri = lax.broadcasted_iota(jnp.int32, (s.lanes, tile), 0)
-            ci = lax.broadcasted_iota(jnp.int32, (s.lanes, tile), 1)
-            goal = first + jnp.where(ci >= F, 1, 0)
-            pick = jnp.where((ri == goal) | (ri == goal + E), 1.0, 0.0).astype(jnp.bfloat16)
-            gate = dot_nn(G[rows, :], pick)
-            pre = dot_nn(X[rows, :], WU[:, cols])
-            value, slope = gelu_and_slope(pre)
+            cols = pl.ds(up((tile0 + n) * tile), tile)
+            gate = gate_tile(rows, tile0 + n)
+            value, slope = gelu_and_slope(dot_nn(X[rows, :], WU[:, cols]))
             HT[rows, cols] = (value * gate).astype(jnp.bfloat16)
             grad_hidden = dot_nt(C[rows, :], WD[cols, :])
             GP[rows, cols] = (grad_hidden * (slope * gate)).astype(jnp.bfloat16)
 
-    def mix(row0, count_rows):
-        rows = pl.ds(up(row0), count_rows)
-
-        @pl.loop(0, D // tile)
+    def forward_units(rows):
+        @pl.loop(0, steps)
         def _(n):
             cols = pl.ds(up(n * tile), tile)
-            MS[rows, cols] = dot_nn(HT[rows, :], WD[:, cols]).astype(jnp.bfloat16)
-
-    def grads(row0, count_rows):
-        rows = pl.ds(up(row0), count_rows)
-
-        @pl.loop(0, D // tile)
+            gate = gate_tile(rows, n)
+            value, slope = gelu_and_slope(dot_nn(X[rows, :], WU[:, cols]))
+            HT[rows, cols] = (value * gate).astype(jnp.bfloat16)
+            SL[:, cols] = slope * gate
+
+    def backward_units(rows):
+        @pl.loop(0, steps)
         def _(n):
             cols = pl.ds(up(n * tile), tile)
-            TS[rows, cols] = dot_nt(GP[rows, :], WU[cols, :]).astype(jnp.bfloat16)
-
-    def give(k, dst, ref, into, send, recv):
-        return remote(block(ref, dst), into.at[pl.ds(up(z * T), T)], send.at[k], recv.at[z], z_peer(dst))
+            GP[rows, cols] = (dot_nt(C[rows, :], WD[cols, :]) * SL[:, cols]).astype(jnp.bfloat16)
+
+    def mix_tile(rows, n):
+        cols = pl.ds(up(n * tile), tile)
+        MS[rows, cols] = dot_nn(HT[rows, :], WD[:, cols]).astype(jnp.bfloat16)
+
+    def grad_tile(rows, n):
+        cols = pl.ds(up(n * tile), tile)
+        TS[rows, cols] = dot_nt(GP[rows, :], WU[cols, :]).astype(jnp.bfloat16)
+
+    sets = ((MS, MN, MP, MR, m_s, m_r), (TS, TN, TP, TR, g_s, g_r))
+
+    def to_near(a):
+        part, into, _, _, send, recv = sets[a]
+        return remote(block(part, near), into, send.at[0], recv.at[0], z_peer(near))
+
+    def to_relay(a, k):
+        part, _, _, into, send, recv = sets[a]
+        return remote(block(part, (second, last)[k]), into.at[k], send.at[1 + k], recv.at[2 + k], z_peer(near))
+
+    def to_far(a, k):
+        part, _, into, _, send, recv = sets[a]
+        goal = (second, last)[k]
+        return remote(block(part, goal), into, send.at[1 + k], recv.at[1], z_peer(goal))
+
+    def pass_on(a, k):
+        part, _, _, into, _, _ = sets[a]
+        to_relay(a, k).wait_recv()
+        rows = pl.ds(up((second, last)[k] * T), T)
+        part[rows, :] = part[rows, :] + into[k]
+        to_far(a, k).start()
 
     own_tok.wait()
     own_cot.wait()
@@ -300,9 +332,9 @@
     def _():
         arrive(3, last, X, tok_s, tok_r)
 
-    near_rows = jnp.where(z < s.n_z // 2, 0, T)
-    count_rows = (s.n_z - 1) * T
-    units(near_rows, count_rows, x * tiles, tiles)
+    most = pl.ds(up(jnp.where(z < s.n_z // 2, 0, T)), (s.n_z - 1) * T)
+    rest = pl.ds(up(last * T), T)
+    units(most, x * tiles)
 
     @pl.when(inner)
     def _():
@@ -311,27 +343,29 @@
     weight_y(3)
     for item in wc_in:
         item.wait_recv()
-    units(near_rows, count_rows, (1 - x) * tiles, tiles)
-    mix(near_rows, count_rows)
-    give(0, near, MS, MR, m_s, m_r).start()
-    give(1, second, MS, MR, m_s, m_r).start()
-    grads(near_rows, count_rows)
-    give(0, near, TS, TR, g_s, g_r).start()
-    give(1, second, TS, TR, g_s, g_r).start()
+    units(most, (1 - x) * tiles)
+
+    @pl.loop(0, steps)
+    def _(n):
+        mix_tile(most, n)
 
     @pl.when(jnp.logical_not(inner))
     def _():
+        to_relay(0, 0).start()
+
+    to_near(0).start()
+
+    @pl.when(jnp.logical_not(inner))
+    def _():
         arrive(3, last, X, tok_s, tok_r)
+
+    forward_units(rest)
+
+    @pl.when(jnp.logical_not(inner))
+    def _():
         arrive(3, last, C, cot_s, cot_r)
 
-    units(last * T, T, 0, s.n_x * tiles)
-    mix(last * T, T)
-    give(2, last, MS, MR, m_s, m_r).start()
-
-    for item in wy_send + wc_send:
-        item.wait_send()
-    Q = WD
-    steps = s.n_x * tiles
+    backward_units(rest)
 
     def unit_rows(i):
         side = jnp.where(i < tiles, 1 - x, x)
@@ -392,7 +426,7 @@
             j = jnp.maximum(i - 1, 0)
             core_copy(j).wait_recv()
             rows = pl.ds(unit_rows(j), tile)
-            Q[rows, :] = (Q[rows, :].astype(jnp.float32) + CR[rows, :].astype(jnp.float32)).astype(jnp.bfloat16)
+            Q[rows, :] = Q[rows, :] + CR[rows, :]
 
             @pl.when(j < tiles)
             def _():
@@ -400,19 +434,45 @@
 
             yd_copy(j).start()
 
+            @pl.when(j < tiles)
+            def _():
+                for k in range(s.n_x):
+                    grad_tile(most, s.n_x * j + k)
+                    mix_tile(rest, s.n_x * j + k)
+
+            @pl.when(j >= tiles)
+            def _():
+                for k in range(s.n_x):
+                    grad_tile(rest, s.n_x * (j - tiles) + k)
+
+            @pl.when((j == tiles - 1) & inner)
+            def _():
+                pass_on(0, 0)
+                to_near(1).start()
+
+            @pl.when((j == tiles - 1) & jnp.logical_not(inner))
+            def _():
+                to_relay(1, 0).start()
+                to_relay(0, 1).start()
+
     core_copy(steps - 2).wait_send()
     core_copy(steps - 1).wait_send()
 
-    grads(last * T, T)
-    give(2, last, TS, TR, g_s, g_r).start()
+    @pl.when(jnp.logical_not(inner))
+    def _():
+        to_relay(1, 1).start()
+        to_near(1).start()
+
+    @pl.when(inner)
+    def _():
+        pass_on(1, 0)
 
     @pl.loop(0, tiles)
     def _(j):
         yd_copy(j).wait_recv()
         rows = pl.ds(up((1 - x) * H + j * tile), tile)
         cols = pl.ds(up(wide + y * sl), sl)
-        got = YD[pl.ds(up(j * tile), tile), :]
-        Q[rows, cols] = (Q[rows, cols].astype(jnp.float32) + got.astype(jnp.float32)).astype(jnp.bfloat16)
+        Q[rows, cols] = Q[rows, cols] + YD[pl.ds(up(j * tile), tile), :]
         xd_copy(j).start()
 
     @pl.loop(0, tiles)
@@ -420,23 +480,36 @@
         xu_copy(j).wait_recv()
         rows = pl.ds(up(x * H + j * tile), tile)
         cols = pl.ds(0, wide)
-        got = XU[pl.ds(up(j * tile), tile), :]
-        Q[rows, cols] = (Q[rows, cols].astype(jnp.float32) + got.astype(jnp.float32)).astype(jnp.bfloat16)
+        Q[rows, cols] = Q[rows, cols] + XU[pl.ds(up(j * tile), tile), :]
         yu_copy(j).start()
 
-    def taken(src, into, recv):
-        remote(block(into, src), block(into, src), recv.at[src], recv.at[src], z_peer(z)).wait_recv()
-
-    def total(out, own, part, into, recv):
-        for src in (near, second, last):
-            taken(src, into, recv)
-        value = own[pl.ds(up(z * T), T), :].astype(jnp.float32) + part[pl.ds(up(z * T), T), :].astype(jnp.float32)
-        for src in (near, second, last):
-            value = value + into[pl.ds(up(src * T), T), :].astype(jnp.float32)
-        out[...] = value.astype(jnp.bfloat16)
-
-    total(mixed_o, X, MS, MR, m_r)
-    total(tgrad_o, C, TS, TR, g_r)
+        @pl.when((j == tiles - 2) & inner)
+        def _():
+            pass_on(0, 1)
+
+    @pl.when(inner)
+    def _():
+        pass_on(1, 1)
+
+    outs = [
+        pltpu.make_async_copy(a, b, osem.at[k])
+        for k, (a, b) in enumerate(((mixed_o, mixed_h), (tgrad_o, tgrad_h), (gup_o, gup_h), (gdown_o, gdown_h)))
+    ]
+
+    def total(a, out, own):
+        part, from_near, from_far, _, _, recv = sets[a]
+        to_near(a).wait_recv()
+        remote(from_far, from_far, recv.at[1], recv.at[1], z_peer(z)).wait_recv()
+        rows = pl.ds(up(z * T), T)
+        out[...] = (
+            own[rows, :].astype(jnp.float32)
+            + part[rows, :].astype(jnp.float32)
+            + from_near[...].astype(jnp.float32)
+            + from_far[...].astype(jnp.float32)
+        ).astype(jnp.bfloat16)
+        outs[a].start()
+
+    total(0, mixed_o, X)
 
     @pl.loop(0, tiles)
     def _(j):
@@ -450,9 +523,11 @@
             + XD[piece, :].astype(jnp.float32)
         ).astype(jnp.bfloat16)
         yu_copy(j).wait_recv()
-        gup_o[piece, :] = (
-            Q[rows, pl.ds(up(y * sl), sl)].astype(jnp.float32) + YU[piece, :].astype(jnp.float32)
-        ).astype(jnp.bfloat16)
+        gup_o[piece, :] = Q[rows, pl.ds(up(y * sl), sl)] + YU[piece, :]
+
+    outs[2].start()
+    outs[3].start()
+    total(1, tgrad_o, C)
 
     @pl.when(has_right)
     def _():
@@ -471,9 +546,12 @@
         gate_copy(k).wait_send()
     for item in wx_send:
         item.wait_send()
-    for k, dst in ((0, near), (1, second), (2, last)):
-        give(k, dst, MS, MR, m_s, m_r).wait_send()
-        give(k, dst, TS, TR, g_s, g_r).wait_send()
+    for item in wy_send + wc_send:
+        item.wait_send()
+    for a in range(2):
+        to_near(a).wait_send()
+        for k in range(2):
+            to_far(a, k).wait_send()
 
     @pl.loop(0, tiles)
     def _(j):
@@ -484,6 +562,31 @@
     @pl.loop(0, steps)
     def _(j):
         yd_copy(j).wait_send()
+
+    for item in outs:
+        item.wait()
+
+
+def finish_kernel(
+    mixed_h, tgrad_h, gup_h, gdown_h, mixed_f, tgrad_f, gup_f, gdown_f, mixed_v, tgrad_v, gup_v, gdown_v, turned, into, out
+):
+    copies = []
+    for k, (a, b) in enumerate(((gup_h, gup_v), (mixed_h, mixed_v), (tgrad_h, tgrad_v), (gdown_h, gdown_v))):
+        copies.append(pltpu.make_async_copy(a, b, into.at[k]))
+        copies[-1].start()
+    back = [
+        pltpu.make_async_copy(a, b, out.at[k])
+        for k, (a, b) in enumerate(((turned, gup_f), (mixed_v, mixed_f), (tgrad_v, tgrad_f), (gdown_v, gdown_f)))
+    ]
+    copies[0].wait()
+    for i in range(gup_v.shape[0]):
+        turned[i] = gup_v[i].T
+    for k in range(1, 4):
+        copies[k].wait()
+        back[k].start()
+    back[0].start()
+    for item in back:
+        item.wait()
 
 
 def per_device(tokens, routes, gates, cotangent, w_up, w_down):
@@ -493,6 +596,7 @@
     wide = s.n_y * s.slice
     n_w = 2 * s.share
     steps = s.n_x * s.tiles
+    block = (s.rows, s.width)
     scratch = [
         pltpu.VMEM((s.column, s.width), bf),
         pltpu.VMEM((s.column, s.width), bf),
@@ -501,27 +605,31 @@
         pltpu.VMEM((s.units, s.width), bf),
         pltpu.VMEM((s.column, s.units), bf),
         pltpu.VMEM((s.column, s.units), bf),
+        pltpu.VMEM((s.rows, s.units), jnp.float32),
         pltpu.VMEM((s.column, s.width), bf),
         pltpu.VMEM((s.column, s.width), bf),
-        pltpu.VMEM((s.column, s.width), bf),
-        pltpu.VMEM((s.column, s.width), bf),
+        pltpu.VMEM(block, bf), pltpu.VMEM(block, bf), pltpu.VMEM((2,) + block, bf),
+        pltpu.VMEM(block, bf), pltpu.VMEM(block, bf), pltpu.VMEM((2,) + block, bf),
+        pltpu.VMEM((s.units, 2 * wide), bf),
         pltpu.VMEM((2, s.tile, 2 * wide), bf),
         pltpu.VMEM((s.units, 2 * wide), bf),
         pltpu.VMEM((s.half, wide), bf),
         pltpu.VMEM((s.units, s.slice), bf),
         pltpu.VMEM((s.half, s.slice), bf),
         pltpu.VMEM((s.half, s.slice), bf),
-        dma((3 + s.local,)),
+        pltpu.VMEM(block, bf), pltpu.VMEM(block, bf),
+        pltpu.VMEM((s.half, s.slice), bf), pltpu.VMEM((s.half, s.slice), bf),
+        pltpu.VMEM((s.top, s.rows), jnp.int32), pltpu.VMEM((s.top, s.rows), jnp.float32),
+        dma((5 + s.local,)), dma((4,)),
         dma((5,)), dma((s.n_z,)), dma((5,)), dma((s.n_z,)), dma((s.n_z,)), dma((s.n_z,)),
         dma((n_w,)), dma((n_w,)), dma((n_w,)), dma((n_w,)), dma((2 * n_w,)), dma((2 * n_w,)),
-        dma((3,)), dma((s.n_z,)), dma((3,)), dma((s.n_z,)),
+        dma((3,)), dma((4,)), dma((3,)), dma((4,)),
         dma((steps,)), dma((steps,)),
         dma((s.tiles,)), dma((s.tiles,)), dma((steps,)), dma((steps,)),
         dma((s.tiles,)), dma((s.tiles,)), dma((s.tiles,)), dma((s.tiles,)),
     ]
     any_space = pl.BlockSpec(memory_space=pl.ANY)
-    vmem = pl.BlockSpec(memory_space=pltpu.VMEM)
-    mixed, token_grad, grad_up, grad_down = pl.pallas_call(
+    parts = pl.pallas_call(
         functools.partial(step_kernel, s),
         out_shape=(
             jax.ShapeDtypeStruct(tokens.shape, bf),
@@ -529,16 +637,38 @@
             jax.ShapeDtypeStruct((s.half, s.slice), bf),
             jax.ShapeDtypeStruct((s.half, s.slice), bf),
         ),
-        in_specs=[any_space, vmem, vmem, any_space, any_space, any_space],
-        out_specs=(vmem, vmem, vmem, vmem),
+        in_specs=[any_space] * 6,
+        out_specs=(any_space,) * 4,
         scratch_shapes=scratch,
         compiler_params=pltpu.CompilerParams(
             collective_id=0, has_side_effects=True, vmem_limit_bytes=67043328
         ),
         name="moe_step",
-    )(tokens, routes, gates, cotangent, w_up, w_down.reshape(s.half, s.width))
-    grad_up = grad_up.reshape(s.local, s.hidden, s.slice).transpose(0, 2, 1)
-    return mixed, token_grad, grad_up, grad_down.reshape(s.local, s.hidden, s.slice)
+    )(tokens, routes.T, gates.T, cotangent, w_up, w_down.reshape(s.half, s.width))
+    shapes = (
+        tokens.shape,
+        tokens.shape,
+        (s.local, s.slice, s.hidden),
+        (s.local, s.hidden, s.slice),
+    )
+    turned = (s.local, s.hidden, s.slice)
+    mixed, token_grad, grad_up, grad_down = parts
+    return pl.pallas_call(
+        finish_kernel,
+        out_shape=tuple(jax.ShapeDtypeStruct(shape, bf) for shape in shapes),
+        in_specs=[any_space] * 4,
+        out_specs=(any_space,) * 4,
+        scratch_shapes=[
+            pltpu.VMEM(tokens.shape, bf),
+            pltpu.VMEM(tokens.shape, bf),
+            pltpu.VMEM(turned, bf),
+            pltpu.VMEM(turned, bf),
+            pltpu.VMEM(shapes[2], bf),
+            dma((4,)),
+            dma((4,)),
+        ],
+        name="finish",
+    )(mixed, token_grad, grad_up.reshape(turned), grad_down.reshape(turned))
 
 
 def per_device_wide(tokens, routes, gates, cotangent, w_up, w_down):

time: 181 us -> 164 us (0.906)
  local copies, waits for them, and re-layouts: 9.91 us -> 0 us
  Pallas kernels: 170 us -> 163 us
    pallas_call x1, Pallas kernels: 170 us -> 160 us  [per_device(): pl.pallas_call(functools.partial(step_kernel, s), out_shape=(jax.ShapeDty...]
    unnamed x7 -> x0, local copies, waits for them, and re-layouts: 7.57 us -> none
    pallas_call x0 -> x1, Pallas kernels: none -> 3.28 us  [per_device(): pl.pallas_call(finish_kernel, out_shape=tuple((jax.ShapeDtypeStruct(shape...]
    reshape x1 -> x0, local copies, waits for them, and re-layouts: 2.35 us -> none  [per_device(): grad_up = grad_up.reshape(s.local, s.hidden, s.slice).transpose(0, 2, 1)]
where the time goes in v1:
time: 164 us
  Pallas kernels  163 us (99%)
    pallas_call x1, Pallas kernels, per_device(): pl.pallas_call(functools.partial(step_kernel, s), out_shape=(jax.ShapeDty...  160 us
    pallas_call x1, Pallas kernels, per_device(): pl.pallas_call(finish_kernel, out_shape=tuple((jax.ShapeDtypeStruct(shape...  3.28 us

profile of v1, /device:TPU:0, one launch (start us, length us, event | category | flops | bytes accessed | tf_op | source)
XLA Modules:
  0.0 163.6 jit_solution(16133174060420582391)
XLA Ops:
  0.6 159.7 %moe_step.1 = (bf16[128,2048]{1,0:T(8,128)(2,1)}, bf16[128,2048]{1,0:T(8,128)(2,1)}, bf16[1024,512]{1,0:T(8,128)(2,1)}, bf16[1024,512]{1,0:T(8,128)(2,1)}) custom-call(bf16[128,2048]{1,0:T(8,128)(2,1)} %tok_h.1, s32[8,128]{1,0:T(8,128)} %bitcast.8, f32[8,128]{1,0:T(8,128)} %bitcast.9, bf16[128,2048]{1,0:T(8,128)(2,1)} %cot_h.1, bf16[8,2048,128]{2,1,0:T(8,128)(2,1)} %up_h.1, ...), custom_call_target="tpu_custom_call" | custom-call | tf_op jit(solution)/shard_map/moe_step/pallas_call | solution.py:632
  160.3 3.3 %finish.1 = (bf16[128,2048]{1,0:T(8,128)(2,1)}, bf16[128,2048]{1,0:T(8,128)(2,1)}, bf16[8,512,128]{2,1,0:T(8,128)(2,1)}, bf16[8,128,512]{2,1,0:T(8,128)(2,1)}) custom-call(bf16[128,2048]{1,0:T(8,128)(2,1)} %get-tuple-element.8.mixed_h, bf16[128,2048]{1,0:T(8,128)(2,1)} %get-tuple-element.9.tgrad_h, bf16[8,128,512]{2,1,0:T(8,128)(2,1)} %bitcast.6, ...), custom_call_target="tpu_custom_call" | custom-call | tf_op jit(solution)/shard_map/finish/pallas_call | solution.py:656

commit v2 on v1

--- a/solution.py
+++ b/solution.py
@@ -130,18 +130,18 @@
     first_x = (y * CORES + c) * s.share
 
     def weight_at(u, x_, base):
-        i = base + u // 2
-        if u % 2 == 0:
-            return WU.at[:, pl.ds(up(x_ * H + i * F), F)]
-        return WD.at[pl.ds(up(x_ * H + i * F), F)]
+        i, half = base + u // 4, u % 2
+        if u % 4 < 2:
+            return WU.at[pl.ds(half * (D // 2), D // 2), pl.ds(up(x_ * H + i * F), F)]
+        return WD.at[pl.ds(pl.multiple_of(x_ * H + i * F + half * (F // 2), F // 2), F // 2)]
 
     def weight_from(u):
-        i = first_x + u // 2
-        if u % 2 == 0:
-            return up_h.at[i]
-        return down_h.at[pl.ds(up(i * F), F)]
-
-    n_w = 2 * s.share
+        i, half = first_x + u // 4, u % 2
+        if u % 4 < 2:
+            return up_h.at[i, pl.ds(half * (D // 2), D // 2)]
+        return down_h.at[pl.ds(pl.multiple_of(i * F + half * (F // 2), F // 2), F // 2)]
+
+    n_w = 4 * s.share
     base_y = ((1 - y) * CORES + c) * s.share
     wx_send = [
         remote(weight_from(u), weight_at(u, x, first_x), wx_s.at[u], wx_r.at[u], x_peer) for u in range(n_w)
@@ -269,19 +269,42 @@
             HT[rows, cols] = (value * gate).astype(jnp.bfloat16)
             SL[:, cols] = slope * gate
 
-    def backward_units(rows):
+    def backward_tile(rows, u0):
+        cols = pl.ds(u0, tile)
+        GP[rows, cols] = (dot_nt(C[rows, :], WD[cols, :]) * SL[:, cols]).astype(jnp.bfloat16)
+
+    def mix_tile(rows, n):
+        cols = pl.ds(up(n * tile), tile)
+        MS[rows, cols] = dot_nn(HT[rows, :], WD[:, cols]).astype(jnp.bfloat16)
+
+    def grad_tile(rows, n):
+        cols = pl.ds(up(n * tile), tile)
+        TS[rows, cols] = dot_nt(GP[rows, :], WU[cols, :]).astype(jnp.bfloat16)
+
+    def mix_side(rows, side, add):
+        inner_cols = pl.ds(up(side * H), H)
+
         @pl.loop(0, steps)
         def _(n):
             cols = pl.ds(up(n * tile), tile)
-            GP[rows, cols] = (dot_nt(C[rows, :], WD[cols, :]) * SL[:, cols]).astype(jnp.bfloat16)
-
-    def mix_tile(rows, n):
+            value = dot_nn(HT[rows, inner_cols], WD[inner_cols, cols])
+            if add:
+                value = value + MS[rows, cols].astype(jnp.float32)
+            MS[rows, cols] = value.astype(jnp.bfloat16)
+
+    def grad_side(rows, side):
+        inner_cols = pl.ds(up(side * H), H)
+
+        @pl.loop(0, steps)
+        def _(n):
+            cols = pl.ds(up(n * tile), tile)
+            TS[rows, cols] = dot_nt(GP[rows, inner_cols], WU[cols, inner_cols]).astype(jnp.bfloat16)
+
+    def grad_rest_tile(rows, side, n):
+        inner_cols = pl.ds(up(side * H), H)
         cols = pl.ds(up(n * tile), tile)
-        MS[rows, cols] = dot_nn(HT[rows, :], WD[:, cols]).astype(jnp.bfloat16)
-
-    def grad_tile(rows, n):
-        cols = pl.ds(up(n * tile), tile)
-        TS[rows, cols] = dot_nt(GP[rows, :], WU[cols, :]).astype(jnp.bfloat16)
+        value = dot_nt(GP[rows, inner_cols], WU[cols, inner_cols]) + TS[rows, cols].astype(jnp.float32)
+        TS[rows, cols] = value.astype(jnp.bfloat16)
 
     sets = ((MS, MN, MP, MR, m_s, m_r), (TS, TN, TP, TR, g_s, g_r))
 
@@ -313,41 +336,72 @@
         item.wait()
     own_down.wait()
 
+    low = z < s.n_z // 2
+    pair = pl.ds(up(jnp.where(low, 0, 2 * T)), 2 * T)
+    single = pl.ds(up(second * T), T)
+    most = pl.ds(up(jnp.where(low, 0, T)), (s.n_z - 1) * T)
+    rest = pl.ds(up(last * T), T)
+
     weight_x(0)
+    weight_x(1)
     arrive(1, near, X, tok_s, tok_r)
-    weight_x(1)
-    arrive(1, near, C, cot_s, cot_r)
     weight_y(0)
-    arrive(2, second, X, tok_s, tok_r)
     weight_x(2)
     weight_y(1)
-    arrive(2, second, C, cot_s, cot_r)
+    weight_x(3)
+    arrive(1, near, C, cot_s, cot_r)
+    weight_y(2)
+
+    @pl.when(inner)
+    def _():
+        arrive(2, second, X, tok_s, tok_r)
+
     gate_in(near)
+    units(pair, x * tiles)
+    weight_x(4)
+    weight_y(3)
+    mix_side(pair, x, False)
+
+    @pl.when(inner)
+    def _():
+        arrive(2, second, C, cot_s, cot_r)
+
+    grad_side(pair, x)
+    weight_x(5)
+    weight_y(4)
+
+    @pl.when(jnp.logical_not(inner))
+    def _():
+        arrive(2, second, X, tok_s, tok_r)
+
+    weight_x(6)
+    weight_y(5)
+
+    @pl.when(inner)
+    def _():
+        arrive(3, last, X, tok_s, tok_r)
+
+    @pl.when(jnp.logical_not(inner))
+    def _():
+        arrive(2, second, C, cot_s, cot_r)
+
+    weight_x(7)
+    weight_y(6)
     gate_in(second)
     gate_in(last)
-    weight_x(3)
-    weight_y(2)
+    units(single, x * tiles)
+    mix_side(single, x, False)
+    grad_side(single, x)
 
     @pl.when(inner)
     def _():
-        arrive(3, last, X, tok_s, tok_r)
-
-    most = pl.ds(up(jnp.where(z < s.n_z // 2, 0, T)), (s.n_z - 1) * T)
-    rest = pl.ds(up(last * T), T)
-    units(most, x * tiles)
-
-    @pl.when(inner)
-    def _():
         arrive(3, last, C, cot_s, cot_r)
 
-    weight_y(3)
+    weight_y(7)
     for item in wc_in:
         item.wait_recv()
     units(most, (1 - x) * tiles)
-
-    @pl.loop(0, steps)
-    def _(n):
-        mix_tile(most, n)
+    mix_side(most, 1 - x, True)
 
     @pl.when(jnp.logical_not(inner))
     def _():
@@ -364,16 +418,17 @@
     @pl.when(jnp.logical_not(inner))
     def _():
         arrive(3, last, C, cot_s, cot_r)
-
-    backward_units(rest)
 
     def unit_rows(i):
         side = jnp.where(i < tiles, 1 - x, x)
         return up(side * H + (i % tiles) * tile)
 
-    def core_copy(i):
-        rows = pl.ds(unit_rows(i), tile)
-        return remote(SB.at[i % 2], CR.at[rows], core_s.at[i], core_r.at[i], c_peer)
+    def core_copy(i, arr):
+        rows, cols = pl.ds(unit_rows(i), tile), pl.ds(arr * wide, wide)
+        return remote(
+            SB.at[i % 2, :, cols], CR.at[rows, cols],
+            core_s.at[arr * steps + i], core_r.at[arr * steps + i], c_peer,
+        )
 
     def xu_copy(i):
         return remote(
@@ -399,64 +454,73 @@
             YU.at[pl.ds(up(j * tile), tile)], yu_s.at[j], yu_r.at[j], y_peer,
         )
 
-    @pl.loop(0, steps + 1)
+    def give_part(i, arr, left_ref, right_ref):
+        @pl.when(i >= 2)
+        def _():
+            core_copy(jnp.maximum(i - 2, 0), arr).wait_send()
+
+        left_t = left_ref[:, pl.ds(unit_rows(i), tile)].T
+        for yy in range(s.n_y):
+            to = pl.ds((arr * s.n_y + yy) * sl, sl)
+            theirs = pl.ds(up((yy * CORES + 1 - c) * sl), sl)
+            SB[i % 2, :, to] = dot_nn(left_t, right_ref[:, theirs]).astype(jnp.bfloat16)
+        core_copy(i, arr).start()
+        return left_t
+
+    def keep_part(i, arr, left_t, right_ref):
+        rows = pl.ds(unit_rows(i), tile)
+        for yy in range(s.n_y):
+            to = pl.ds((arr * s.n_y + yy) * sl, sl)
+            mine = pl.ds(up((yy * CORES + c) * sl), sl)
+            Q[rows, to] = dot_nn(left_t, right_ref[:, mine]).astype(jnp.bfloat16)
+
+    def join(i, arr):
+        core_copy(i, arr).wait_recv()
+        rows, cols = pl.ds(unit_rows(i), tile), pl.ds(arr * wide, wide)
+        Q[rows, cols] = Q[rows, cols] + CR[rows, cols]
+
+    @pl.loop(0, steps)
     def _(i):
-        @pl.when(i < steps)
+        hid_t = give_part(i, 1, HT, C)
+        backward_tile(rest, unit_rows(i))
+        grad_t = give_part(i, 0, GP, X)
+        keep_part(i, 1, hid_t, C)
+        join(i, 1)
+        yd_copy(i).start()
+        keep_part(i, 0, grad_t, X)
+        join(i, 0)
+
+        @pl.when(i < tiles)
         def _():
-            @pl.when(i >= 2)
-            def _():
-                core_copy(jnp.maximum(i - 2, 0)).wait_send()
-
-            r0 = unit_rows(i)
-            rows = pl.ds(r0, tile)
-            slot = i % 2
-            grad_t = GP[:, rows].T
-            hid_t = HT[:, rows].T
-            for yy in range(s.n_y):
-                for arr, (left_t, right_ref) in enumerate(((grad_t, X), (hid_t, C))):
-                    to = pl.ds((arr * s.n_y + yy) * sl, sl)
-                    theirs = pl.ds(up((yy * CORES + 1 - c) * sl), sl)
-                    mine = pl.ds(up((yy * CORES + c) * sl), sl)
-                    SB[slot, :, to] = dot_nn(left_t, right_ref[:, theirs]).astype(jnp.bfloat16)
-                    Q[rows, to] = dot_nn(left_t, right_ref[:, mine]).astype(jnp.bfloat16)
-            core_copy(i).start()
-
-        @pl.when(i >= 1)
+            xu_copy(i).start()
+            for k in range(s.n_x):
+                grad_rest_tile(most, 1 - x, s.n_x * i + k)
+
+        @pl.when(i >= tiles)
         def _():
-            j = jnp.maximum(i - 1, 0)
-            core_copy(j).wait_recv()
-            rows = pl.ds(unit_rows(j), tile)
-            Q[rows, :] = Q[rows, :] + CR[rows, :]
-
-            @pl.when(j < tiles)
-            def _():
-                xu_copy(j).start()
-
-            yd_copy(j).start()
-
-            @pl.when(j < tiles)
-            def _():
-                for k in range(s.n_x):
-                    grad_tile(most, s.n_x * j + k)
-                    mix_tile(rest, s.n_x * j + k)
-
-            @pl.when(j >= tiles)
-            def _():
-                for k in range(s.n_x):
-                    grad_tile(rest, s.n_x * (j - tiles) + k)
-
-            @pl.when((j == tiles - 1) & inner)
-            def _():
-                pass_on(0, 0)
-                to_near(1).start()
-
-            @pl.when((j == tiles - 1) & jnp.logical_not(inner))
-            def _():
-                to_relay(1, 0).start()
-                to_relay(0, 1).start()
-
-    core_copy(steps - 2).wait_send()
-    core_copy(steps - 1).wait_send()
+            for k in range(s.n_x):
+                mix_tile(rest, s.n_x * (i - tiles) + k)
+
+        @pl.when((i == tiles - 1) & inner)
+        def _():
+            to_near(1).start()
+            pass_on(0, 0)
+
+        @pl.when((i == tiles - 1) & jnp.logical_not(inner))
+        def _():
+            to_relay(1, 0).start()
+
+    for k in range(2):
+        core_copy(steps - 2 + k, 0).wait_send()
+        core_copy(steps - 2 + k, 1).wait_send()
+
+    @pl.when(jnp.logical_not(inner))
+    def _():
+        to_relay(0, 1).start()
+
+    @pl.loop(0, steps)
+    def _(n):
+        grad_tile(rest, n)
 
     @pl.when(jnp.logical_not(inner))
     def _():
@@ -483,12 +547,9 @@
         Q[rows, cols] = Q[rows, cols] + XU[pl.ds(up(j * tile), tile), :]
         yu_copy(j).start()
 
-        @pl.when((j == tiles - 2) & inner)
-        def _():
-            pass_on(0, 1)
-
     @pl.when(inner)
     def _():
+        pass_on(0, 1)
         pass_on(1, 1)
 
     outs = [
@@ -594,7 +655,7 @@
     bf = jnp.bfloat16
     dma = pltpu.SemaphoreType.DMA
     wide = s.n_y * s.slice
-    n_w = 2 * s.share
+    n_w = 4 * s.share
     steps = s.n_x * s.tiles
     block = (s.rows, s.width)
     scratch = [
@@ -624,7 +685,7 @@
         dma((5,)), dma((s.n_z,)), dma((5,)), dma((s.n_z,)), dma((s.n_z,)), dma((s.n_z,)),
         dma((n_w,)), dma((n_w,)), dma((n_w,)), dma((n_w,)), dma((2 * n_w,)), dma((2 * n_w,)),
         dma((3,)), dma((4,)), dma((3,)), dma((4,)),
-        dma((steps,)), dma((steps,)),
+        dma((2 * steps,)), dma((2 * steps,)),
         dma((s.tiles,)), dma((s.tiles,)), dma((steps,)), dma((steps,)),
         dma((s.tiles,)), dma((s.tiles,)), dma((s.tiles,)), dma((s.tiles,)),
     ]

time: 164 us -> 158 us (0.963)
  Pallas kernels: 163 us -> 158 us
    pallas_call x1, Pallas kernels: 160 us -> 154 us  [per_device(): pl.pallas_call(functools.partial(step_kernel, s), out_shape=(jax.ShapeDty...]
where the time goes in v2:
time: 158 us
  Pallas kernels  158 us (100%)
    pallas_call x1, Pallas kernels, per_device(): pl.pallas_call(functools.partial(step_kernel, s), out_shape=(jax.ShapeDty...  154 us
    pallas_call x1, Pallas kernels, per_device(): pl.pallas_call(finish_kernel, out_shape=tuple((jax.ShapeDtypeStruct(shape...  3.28 us

profile of v2, /device:TPU:0, one launch (start us, length us, event | category | flops | bytes accessed | tf_op | source)
XLA Modules:
  0.0 158.2 jit_solution(1097705929264605357)
XLA Ops:
  0.6 154.2 %moe_step.1 = (bf16[128,2048]{1,0:T(8,128)(2,1)}, bf16[128,2048]{1,0:T(8,128)(2,1)}, bf16[1024,512]{1,0:T(8,128)(2,1)}, bf16[1024,512]{1,0:T(8,128)(2,1)}) custom-call(bf16[128,2048]{1,0:T(8,128)(2,1)} %tok_h.1, s32[8,128]{1,0:T(8,128)} %bitcast.8, f32[8,128]{1,0:T(8,128)} %bitcast.9, bf16[128,2048]{1,0:T(8,128)(2,1)} %cot_h.1, bf16[8,2048,128]{2,1,0:T(8,128)(2,1)} %up_h.1, ...), custom_call_target="tpu_custom_call" | custom-call | tf_op jit(solution)/shard_map/moe_step/pallas_call | solution.py:693
  154.9 3.3 %finish.1 = (bf16[128,2048]{1,0:T(8,128)(2,1)}, bf16[128,2048]{1,0:T(8,128)(2,1)}, bf16[8,512,128]{2,1,0:T(8,128)(2,1)}, bf16[8,128,512]{2,1,0:T(8,128)(2,1)}) custom-call(bf16[128,2048]{1,0:T(8,128)(2,1)} %get-tuple-element.8.mixed_h, bf16[128,2048]{1,0:T(8,128)(2,1)} %get-tuple-element.9.tgrad_h, bf16[8,128,512]{2,1,0:T(8,128)(2,1)} %bitcast.6, ...), custom_call_target="tpu_custom_call" | custom-call | tf_op jit(solution)/shard_map/finish/pallas_call | solution.py:717

commit v3 on v2

--- a/solution.py
+++ b/solution.py
@@ -93,7 +93,7 @@
         )
 
     def up(n):
-        return pl.multiple_of(n, 128)
+        return n if isinstance(n, int) else pl.multiple_of(n, 128)
 
     def block(ref, zz):
         return ref.at[pl.ds(up(zz * T), T)]
@@ -381,12 +381,13 @@
     def _():
         arrive(3, last, X, tok_s, tok_r)
 
-    @pl.when(jnp.logical_not(inner))
-    def _():
-        arrive(2, second, C, cot_s, cot_r)
-
     weight_x(7)
     weight_y(6)
+
+    @pl.when(jnp.logical_not(inner))
+    def _():
+        arrive(2, second, C, cot_s, cot_r)
+
     gate_in(second)
     gate_in(last)
     units(single, x * tiles)
@@ -554,8 +555,13 @@
 
     outs = [
         pltpu.make_async_copy(a, b, osem.at[k])
-        for k, (a, b) in enumerate(((mixed_o, mixed_h), (tgrad_o, tgrad_h), (gup_o, gup_h), (gdown_o, gdown_h)))
-    ]
+        for k, (a, b) in enumerate(((mixed_o, mixed_h), (tgrad_o, tgrad_h)))
+    ]
+
+    def weight_out(j, k):
+        piece = pl.ds(up(j * tile), tile)
+        a, b = ((gup_o, gup_h), (gdown_o, gdown_h))[k]
+        return pltpu.make_async_copy(a.at[piece], b.at[piece], osem.at[2 + 2 * j + k])
 
     def total(a, out, own):
         part, from_near, from_far, _, _, recv = sets[a]
@@ -572,8 +578,7 @@
 
     total(0, mixed_o, X)
 
-    @pl.loop(0, tiles)
-    def _(j):
+    def last_sum(j):
         yd_copy(tiles + j).wait_recv()
         xd_copy(j).wait_recv()
         rows = pl.ds(up(x * H + j * tile), tile)
@@ -584,11 +589,16 @@
             + XD[piece, :].astype(jnp.float32)
         ).astype(jnp.bfloat16)
         yu_copy(j).wait_recv()
+        weight_out(j, 1).start()
         gup_o[piece, :] = Q[rows, pl.ds(up(y * sl), sl)] + YU[piece, :]
-
-    outs[2].start()
-    outs[3].start()
+        weight_out(j, 0).start()
+
+    @pl.loop(0, tiles - 1)
+    def _(j):
+        last_sum(j)
+
     total(1, tgrad_o, C)
+    last_sum(tiles - 1)
 
     @pl.when(has_right)
     def _():
@@ -626,6 +636,11 @@
 
     for item in outs:
         item.wait()
+
+    @pl.loop(0, tiles)
+    def _(j):
+        weight_out(j, 0).wait()
+        weight_out(j, 1).wait()
 
 
 def finish_kernel(
@@ -681,7 +696,7 @@
         pltpu.VMEM(block, bf), pltpu.VMEM(block, bf),
         pltpu.VMEM((s.half, s.slice), bf), pltpu.VMEM((s.half, s.slice), bf),
         pltpu.VMEM((s.top, s.rows), jnp.int32), pltpu.VMEM((s.top, s.rows), jnp.float32),
-        dma((5 + s.local,)), dma((4,)),
+        dma((5 + s.local,)), dma((2 + 2 * s.tiles,)),
         dma((5,)), dma((s.n_z,)), dma((5,)), dma((s.n_z,)), dma((s.n_z,)), dma((s.n_z,)),
         dma((n_w,)), dma((n_w,)), dma((n_w,)), dma((n_w,)), dma((2 * n_w,)), dma((2 * n_w,)),
         dma((3,)), dma((4,)), dma((3,)), dma((4,)),

time: 158 us -> 158 us (level)
  no operation moved by 1% of the time
where the time goes in v3:
time: 158 us
  Pallas kernels  157 us (99%)
    pallas_call x1, Pallas kernels, per_device(): pl.pallas_call(functools.partial(step_kernel, s), out_shape=(jax.ShapeDty...  154 us
    pallas_call x1, Pallas kernels, per_device(): pl.pallas_call(finish_kernel, out_shape=tuple((jax.ShapeDtypeStruct(shape...  3.28 us

profile of v3, /device:TPU:0, one launch (start us, length us, event | category | flops | bytes accessed | tf_op | source)
XLA Modules:
  0.0 157.5 jit_solution(6125765805633758580)
XLA Ops:
  0.6 153.6 %moe_step.1 = (bf16[128,2048]{1,0:T(8,128)(2,1)}, bf16[128,2048]{1,0:T(8,128)(2,1)}, bf16[1024,512]{1,0:T(8,128)(2,1)}, bf16[1024,512]{1,0:T(8,128)(2,1)}) custom-call(bf16[128,2048]{1,0:T(8,128)(2,1)} %tok_h.1, s32[8,128]{1,0:T(8,128)} %bitcast.8, f32[8,128]{1,0:T(8,128)} %bitcast.9, bf16[128,2048]{1,0:T(8,128)(2,1)} %cot_h.1, bf16[8,2048,128]{2,1,0:T(8,128)(2,1)} %up_h.1, ...), custom_call_target="tpu_custom_call" | custom-call | tf_op jit(solution)/shard_map/moe_step/pallas_call | solution.py:708
  154.2 3.3 %finish.1 = (bf16[128,2048]{1,0:T(8,128)(2,1)}, bf16[128,2048]{1,0:T(8,128)(2,1)}, bf16[8,512,128]{2,1,0:T(8,128)(2,1)}, bf16[8,128,512]{2,1,0:T(8,128)(2,1)}) custom-call(bf16[128,2048]{1,0:T(8,128)(2,1)} %get-tuple-element.8.mixed_h, bf16[128,2048]{1,0:T(8,128)(2,1)} %get-tuple-element.9.tgrad_h, bf16[8,128,512]{2,1,0:T(8,128)(2,1)} %bitcast.6, ...), custom_call_target="tpu_custom_call" | custom-call | tf_op jit(solution)/shard_map/finish/pallas_call | solution.py:732
